TPU v7x, 32 devices: a whole 2x2x4 slice. The times are simulated.
32 devices in a mesh: ctx: 8 (over z, x), head: 4 (over y, core).
Axes of the slice: x: 2, y: 2, z: 4, core: 2. Of those that a mesh axis runs over, the one named last changes fastest.
Arguments:
- positions: int32 [128], replicated, may hold values from 1 to 8191, as said below
- mla_queries: bfloat16 [128, 128, 576], P(None, 'head'), may hold values from -5000 to 5000
- latent_keys: bfloat16 [8192, 576], P('ctx'), may hold values from -18 to 18
- index_queries: bfloat16 [128, 64, 128], P(None, 'head'), may hold values from -64 to 64
- index_keys: bfloat16 [8192, 128], P('ctx'), may hold values from -18 to 18
- head_weights: float32 [128, 64], P(None, 'head'), may hold values from -4 to 4
Outputs:
- grad_queries: float32 [128, 64, 128], P('ctx', 'head')
- grad_keys: float32 [8192, 128], P(('ctx', 'head'))
- grad_weights: float32 [128, 64], P('ctx', 'head')
Inputs may be any that keep to these rules, and one draw needn't show every extreme that they name: Each query sees the keys at positions 0 to its own position.
All inputs are finite; a program needn't handle non-finite values.
Results may differ from a plain program's by a relative error of at most 0.0045.
Values may be sent and summed in bfloat16 or wider, within the bound.
A program may use at most 128 MiB of HBM per device.

v0:
```python
import math

import jax
import jax.numpy as jnp
from jax import lax
from jax.sharding import PartitionSpec as P

HEADS = 128
QK_HEAD = 192


masked_value = -1e30


def masked_highest(values, allowed):
    return jnp.max(jnp.where(allowed, values, masked_value), axis=-1)


def shifted_exp(values, allowed, highest):
    return jnp.where(allowed, jnp.exp(values - highest[..., None]), 0.0)


def local(positions, mla_queries, latent_keys, index_queries, index_keys, head_weights):
    rows = latent_keys.shape[0]
    key_pos = lax.axis_index("ctx") * rows + jnp.arange(rows, dtype=jnp.int32)
    allowed = key_pos[None, :] <= positions[:, None]
    scores = jnp.einsum(
        "thd,sd->hts", mla_queries, latent_keys, preferred_element_type=jnp.float32
    ) * (1.0 / math.sqrt(QK_HEAD))
    head_mask = allowed[None]
    highest = lax.pmax(masked_highest(scores, head_mask), "ctx")
    exponent = shifted_exp(scores, head_mask, highest)
    totals = lax.psum(jnp.sum(exponent, axis=-1), "ctx")
    factor = 1.0 / totals
    mla_part = jnp.sum(exponent * factor[..., None], axis=0)
    inner = jnp.einsum("tjd,sd->tjs", index_queries, index_keys, preferred_element_type=jnp.float32)
    active = jnp.maximum(inner, 0.0)
    logit_part = jnp.einsum("tj,tjs->ts", head_weights, active, precision=lax.Precision.HIGHEST)
    target, logits = (
        lax.psum_scatter(mla_part, "head", scatter_dimension=0, tiled=True),
        lax.psum_scatter(logit_part, "head", scatter_dimension=0, tiled=True),
    )
    share = target.shape[0]
    row_mask = lax.dynamic_slice_in_dim(allowed, lax.axis_index("head") * share, share, 0)
    target = target / HEADS
    index_high = lax.pmax(masked_highest(logits, row_mask), "ctx")
    index_exp = shifted_exp(logits, row_mask, index_high)
    index_sum = lax.psum(jnp.sum(index_exp, axis=-1), "ctx")
    index_factor = 1.0 / index_sum
    predicted = index_exp * index_factor[:, None]
    gradient = jnp.where(
        row_mask, math.sqrt(rows * lax.axis_size("ctx")) * (predicted - target), 0.0
    ).astype(jnp.bfloat16)
    gradient = lax.all_gather(gradient, "head", axis=0, tiled=True)
    grad_float = gradient.astype(jnp.float32)
    weight_part = jnp.einsum("ts,tjs->tj", grad_float, active, precision=lax.Precision.HIGHEST)
    delta = jnp.where(inner > 0, grad_float[:, None, :] * head_weights[:, :, None], 0.0).astype(
        jnp.bfloat16
    )
    query_part = jnp.einsum("tjs,sd->tjd", delta, index_keys, preferred_element_type=jnp.float32)
    grad_queries, grad_weights = (
        lax.psum_scatter(query_part, "ctx", scatter_dimension=0, tiled=True),
        lax.psum_scatter(weight_part, "ctx", scatter_dimension=0, tiled=True),
    )
    grad_keys = lax.psum_scatter(
        jnp.einsum("tjs,tjd->sd", delta, index_queries, preferred_element_type=jnp.float32),
        "head",
        scatter_dimension=0,
        tiled=True,
    )
    return (grad_queries, grad_keys, grad_weights)


def solution(mesh):
    in_specs = (
        P(),
        P(None, "head", None),
        P("ctx", None),
        P(None, "head", None),
        P("ctx", None),
        P(None, "head"),
    )
    out_specs = (P("ctx", "head", None), P(("ctx", "head"), None), P("ctx", "head"))
    return jax.shard_map(local, mesh=mesh, in_specs=in_specs, out_specs=out_specs, check_vma=False)
```

profile of v0, /device:TPU:0, one launch (start us, length us, event | category | flops | bytes accessed | tf_op | source)
XLA Modules:
  0.0 318.5 jit_solution(9850725890422266074)
XLA Ops:
  7.2 0.0 copy-start
  7.2 0.0 copy-start.5
  7.2 0.0 reduce-scatter.16.cloned.1.call-start
  7.2 9.4 %broadcast_maximum_fusion = (f32[128,16,1024]{2,0,1:T(8,128)}, f32[128,1024]{1,0:T(8,128)}, f32[128,16,1024]{2,0,1:T(8,128)}) fusion(f32[128,16]{0,1:T(8,128)} %param.11, bf16[1024,128]{1,0:T(8,128)(2,1)} %param.10, bf16[128,16,128]{2,1,0:T(8,128)(2,1)} %param.9), kind=kOutput, calls=%fused_computation.24 | convolution fusion | flops 543031296 | bytes 18096128 | tf_op jit(solution)/shard_map/tjd,sd->tjs/dot_general | solution.py:36
  16.6 0.0 reduce-scatter.16.cloned.1.call-update
  16.6 0.0 reduce-scatter.18.cloned.1.call-start
  16.7 0.0 copy-done.5
  16.7 0.1 broadcast_compare_fusion
  16.9 0.3 copy.27
  17.1 0.0 copy-done
  17.1 13.1 %fusion = (f32[32,128]{1,0:T(8,128)S(1)}, f32[1024,128,32]{1,0,2:T(8,128)}) fusion(pred[128,1024]{0,1:T(8,128)(4,1)S(1)} %copy.27, bf16[128,32,576]{0,2,1:T(8,128)(2,1)} %param.7, bf16[1024,576]{0,1:T(8,128)(2,1)S(1)} %copy-done), kind=kOutput, calls=%fused_computation.2 | convolution fusion | flops 4844417024 | bytes 22822912 | tf_op jit(solution)/shard_map/thd,sd->hts/dot_general | solution.py:27
  30.3 10.9 %reduce-scatter.16.cloned.1.call-done = f32[32,1024]{1,0:T(8,128)} async-done(((f32[128,1024]{1,0:T(8,128)}), f32[32,1024]{1,0:T(8,128)}) %reduce-scatter.16.cloned.1.call-update) | async-done | bytes 131088 | tf_op jit(solution)/shard_map/reduce_scatter | solution.py:41
  41.2 1.0 select_reduce_fusion
  42.2 37.1 %all-reduce.1 = (f32[32,128]{1,0:T(8,128)S(1)}, f32[32]{0:T(128)S(1)}) all-reduce(f32[32,128]{1,0:T(8,128)S(1)} %get-tuple-element.21, f32[32]{0:T(128)S(1)} %select_reduce_fusion), channel_id=1, replica_groups=mesh['ctx'=8,'head'=4] {'ctx'}, use_global_device_ids=true, to_apply=%region_6.7 | all-reduce | flops 4128 | bytes 33024 | tf_op jit(solution)/shard_map/pmax | solution.py:31
  79.3 0.0 copy-start.1
  79.3 9.1 %fusion.3 = f32[32,128]{1,0:T(8,128)S(1)} fusion(f32[1024,128,32]{1,0,2:T(8,128)} %get-tuple-element.22, f32[32,128]{1,0:T(8,128)S(1)} %get-tuple-element.17, pred[128,1024]{0,1:T(8,128)(4,1)S(1)} %copy.27), kind=kLoop, calls=%fused_computation.6 | loop fusion | flops 16773120 | bytes 16941056 | tf_op jit(solution)/shard_map/reduce_sum | solution.py:33
  88.4 0.0 copy-done.1
  88.4 0.2 fusion.28
  88.6 33.0 %all-reduce = (f32[32,128]{1,0:T(8,128)S(1)}, f32[32]{0:T(128)S(1)}) all-reduce(f32[32,128]{1,0:T(8,128)S(1)} %fusion.3, f32[32]{0:T(128)S(1)} %fusion.28), channel_id=1, replica_groups=mesh['ctx'=8,'head'=4] {'ctx'}, use_global_device_ids=true, to_apply=%region_8.9 | all-reduce | flops 4128 | bytes 33024 | tf_op jit(solution)/shard_map/psum | solution.py:33
  121.7 8.0 %multiply_reduce_fusion = f32[128,1024]{0,1:T(8,128)S(1)} fusion(f32[1024,128,32]{1,0,2:T(8,128)} %get-tuple-element.22, f32[32,128]{1,0:T(8,128)S(1)} %broadcast_divide_fusion, f32[32,128]{1,0:T(8,128)S(1)} %get-tuple-element.17, pred[128,1024]{0,1:T(8,128)(4,1)S(1)} %copy.27), kind=kLoop, calls=%fused_computation.5 | loop fusion | flops 20840448 | bytes 17465344 | tf_op jit(solution)/shard_map/reduce_sum | solution.py:35
  129.7 0.0 copy-start.3
  129.7 0.0 copy-start.4
  129.7 1.0 copy.43
  130.7 0.0 reduce-scatter.18.cloned.1.call-update
  130.7 0.2 reduce-scatter.10.cloned.1.call-start
  130.9 4.6 %fusion.8 = u16[128,1024]{1,0:T(8,128)(2,1)S(1)} fusion(f32[128,16,1024]{2,0,1:T(8,128)} %get-tuple-element.23), kind=kLoop, calls=%fused_computation.15 | loop fusion | flops 10354688 | bytes 8650752
  135.6 13.3 %reduce-scatter.18.cloned.1.call-done = f32[32,1024]{1,0:T(8,128)} async-done(((f32[128,1024]{1,0:T(8,128)}), f32[32,1024]{1,0:T(8,128)}) %reduce-scatter.18.cloned.1.call-update) | async-done | bytes 131088 | tf_op jit(solution)/shard_map/reduce_scatter | solution.py:40
  148.8 1.0 select_convert_fusion.5
  149.9 5.8 %all_gather.3 = bf16[128,1024]{1,0:T(8,128)(2,1)S(1)} all-gather(bf16[32,1024]{1,0:T(8,128)(2,1)S(1)} %select_convert_fusion.5), channel_id=1, replica_groups=mesh['ctx'=8,'head'=4] {'head'}, dimensions={0}, use_global_device_ids=true | all-gather | bytes 327680 | tf_op jit(solution)/shard_map/all_gather | solution.py:54
  155.7 0.0 copy-done.3
  155.7 0.0 copy-done.4
  155.7 2.4 fusion.7
  158.1 0.0 copy-start.2
  158.1 0.0 reduce-scatter.10.cloned.1.call-update
  158.1 0.0 reduce-scatter.14.cloned.1.call-start
  158.2 13.6 %fusion.4 = f32[128,1,16]{2,1,0:T(1,128)} fusion(f32[128,16,1024]{2,0,1:T(8,128)} %get-tuple-element.19, bf16[128,1024,1]{1,0,2:T(8,128)(2,1)S(1)} %bitcast.33), kind=kOutput, calls=%fused_computation.9 | convolution fusion | flops 25165824 | bytes 8658944 | tf_op jit(solution)/shard_map/ts,tjs->tj/dot_general | solution.py:56
  171.7 0.0 reduce-scatter.14.cloned.1.call-update
  171.8 0.0 reduce-scatter.12.cloned.1.call-start
  171.8 0.0 copy-done.2
  171.8 2.8 fusion.19
  174.7 0.0 reduce-scatter.12.cloned.1.call-update
  174.7 48.2 %reduce-scatter.10.cloned.1.call-done = f32[16,16,128]{2,0,1:T(8,128)} async-done(((f32[128,16,128]{2,0,1:T(8,128)}), f32[16,16,128]{2,0,1:T(8,128)}) %reduce-scatter.10.cloned.1.call-update) | async-done | bytes 131088 | tf_op jit(solution)/shard_map/reduce_scatter | solution.py:62
  223.0 1.6 copy.31
  224.6 63.7 %reduce-scatter.14.cloned.1.call-done = f32[16,16]{1,0:T(8,128)} async-done(((f32[128,16]{1,0:T(8,128)}), f32[16,16]{1,0:T(8,128)}) %reduce-scatter.14.cloned.1.call-update) | async-done | bytes 1040 | tf_op jit(solution)/shard_map/reduce_scatter | solution.py:63
  288.2 23.7 %reduce-scatter.12.cloned.1.call-done = f32[256,128]{1,0:T(8,128)} async-done(((f32[1024,128]{1,0:T(8,128)}), f32[256,128]{1,0:T(8,128)}) %reduce-scatter.12.cloned.1.call-update) | async-done | bytes 131088 | tf_op jit(solution)/shard_map/reduce_scatter | solution.py:65
  (4 shorter events, 0.1 us)
Async XLA Ops:
  7.2 10.0 %copy-start = (bf16[1024,576]{0,1:T(8,128)(2,1)S(1)}, bf16[1024,576]{0,1:T(8,128)(2,1)}, u32[]{:S(2)}) copy-start(bf16[1024,576]{0,1:T(8,128)(2,1)} %param.8) | copy-start | bytes 3538948
  7.2 9.5 %copy-start.5 = (s32[128]{0:T(128)S(1)}, s32[128]{0:T(128)}, u32[]{:S(2)}) copy-start(s32[128]{0:T(128)} %param.6) | copy-start | bytes 1540
  7.2 34.0 %reduce-scatter.16.cloned.1.call-start = ((), (), s32[]{:S(2)}) async-start(), calls=%async_computation.8 | async-start | bytes 655360 | tf_op jit(solution)/shard_map/reduce_scatter | solution.py:41
  16.6 132.2 %reduce-scatter.18.cloned.1.call-start = ((), (), s32[]{:S(2)}) async-start(), calls=%async_computation.9 | async-start | bytes 655360 | tf_op jit(solution)/shard_map/reduce_scatter | solution.py:40
  79.3 9.1 %copy-start.1 = (f32[32,1024]{1,0:T(8,128)S(1)}, f32[32,1024]{1,0:T(8,128)}, u32[]{:S(2)}) copy-start(f32[32,1024]{1,0:T(8,128)} %reduce-scatter.16.cloned.1.call-done) | copy-start | bytes 393220
  129.7 26.0 %copy-start.3 = (bf16[1024,128]{1,0:T(8,128)(2,1)S(1)}, bf16[1024,128]{1,0:T(8,128)(2,1)}, u32[]{:S(2)}) copy-start(bf16[1024,128]{1,0:T(8,128)(2,1)} %param.10) | copy-start | bytes 786436
  129.7 26.0 %copy-start.4 = (f32[128,16]{0,1:T(8,128)S(1)}, f32[128,16]{0,1:T(8,128)}, u32[]{:S(2)}) copy-start(f32[128,16]{0,1:T(8,128)} %param.11) | copy-start | bytes 24580
  130.7 92.2 %reduce-scatter.10.cloned.1.call-start = ((), (), s32[]{:S(2)}) async-start(), calls=%async_computation.5 | async-start | bytes 1179648 | tf_op jit(solution)/shard_map/reduce_scatter | solution.py:62
  158.1 13.7 %copy-start.2 = (bf16[128,16,128]{2,1,0:T(8,128)(2,1)S(1)}, bf16[128,16,128]{2,1,0:T(8,128)(2,1)}, u32[]{:S(2)}) copy-start(bf16[128,16,128]{2,1,0:T(8,128)(2,1)} %param.9) | copy-start | bytes 1572868
  158.1 130.1 %reduce-scatter.14.cloned.1.call-start = ((), (), s32[]{:S(2)}) async-start(), calls=%async_computation.7 | async-start | bytes 73728 | tf_op jit(solution)/shard_map/reduce_scatter | solution.py:63
  171.8 140.2 %reduce-scatter.12.cloned.1.call-start = ((), (), s32[]{:S(2)}) async-start(), calls=%async_computation.6 | async-start | bytes 655360 | tf_op jit(solution)/shard_map/reduce_scatter | solution.py:65
Sparse Core Ops, SparseCore 0:
  16.8 24.3 reduce-scatter.15
  130.8 17.9 reduce-scatter.17
  158.2 64.6 reduce-scatter.9
  226.8 61.4 reduce-scatter.13
  291.2 20.7 reduce-scatter.11
where the time goes:
time: 319 us; the launch traced here: 318 us
  waiting for transfers between devices  160 us (50%)
  blocking collectives  75.9 us (24%)
  matrix products  41.3 us (13%)
  other arithmetic  24.2 us (8%)
  between operations  13.9 us (4%)
    reduce_scatter x1, waiting for transfers between devices, local(): lax.psum_scatter(weight_part, 'ctx', scatter_dimension=0, tiled=True)  63.7 us
    reduce_scatter x1, waiting for transfers between devices, local(): lax.psum_scatter(query_part, 'ctx', scatter_dimension=0, tiled=True)  48.2 us
    pmax x1, blocking collectives, local(): highest = lax.pmax(masked_highest(scores, head_mask), 'ctx')  37.1 us
    psum x1, blocking collectives, local(): totals = lax.psum(jnp.sum(exponent, axis=-1), 'ctx')  33 us
    reduce_scatter x1, waiting for transfers between devices, local(): lax.psum_scatter(jnp.einsum('tjs,tjd->sd', delta, index_queries, preferre...  23.7 us
    dot_general x1, matrix products, local(): jnp.einsum('ts,tjs->tj', grad_float, active, precision=lax.Precision.HIGH...  13.6 us
    reduce_scatter x1, waiting for transfers between devices, local(): lax.psum_scatter(mla_part, 'head', scatter_dimension=0, tiled=True)  13.3 us
    dot_general x1, matrix products, local(): jnp.einsum('thd,sd->hts', mla_queries, latent_keys, preferred_element_typ...  13.1 us
  transfers between devices with their start and end apart: 5, of which 5 were waited for; matrix products, arithmetic and copies ran while one was open for 11% of the time, Pallas kernels for 0%

commit v1 on v0

v1 whole, which is shorter than its diff:
```python
import functools
import math

import jax
import jax.numpy as jnp
from jax import lax
from jax.experimental import pallas as pl
from jax.experimental.pallas import tpu as pltpu
from jax.sharding import PartitionSpec as P

HEADS = 128
QK_HEAD = 192
LANES = 256
GROUP = 4
MESH = pl.DeviceIdType.MESH
F32 = jnp.float32
BF16 = jnp.bfloat16
MASKED = -1e30
FLOOR = -1e20
LOG2E = math.log2(math.e)
NT = (((1,), (1,)), ((), ()))


def dot(a, b):
    return jnp.dot(a, b, preferred_element_type=F32)


def dot_nt(a, b):
    return lax.dot_general(a, b, NT, preferred_element_type=F32)


def iota(shape, dim):
    return lax.broadcasted_iota(jnp.int32, shape, dim)


def spread(shape, query_dim, width, first):
    query = iota(shape, query_dim) * width
    lane = iota(shape, 1 - query_dim) + first
    return (query <= lane) & (lane < query + width)


def start_all(axis, n, me, source, slot, send, recv):
    copies = []
    for o in range(1, n):
        dest = lax.rem(me + o, n)
        copy = pltpu.make_async_remote_copy(
            src_ref=source(dest),
            dst_ref=slot(o),
            send_sem=send.at[o],
            recv_sem=recv.at[o],
            device_id={axis: dest},
            device_id_type=MESH,
        )
        copy.start()
        copies.append(copy)
    return copies


def kernel(
    nc, nh, hl, jl, queries,
    q_hbm, latt_ref, iq_ref, ik_ref, w_ref, pos_ref,
    gq_out, gk_out, gw_out,
    q_buf, e_buf, inner_buf, lg_part, lg_recv, lgq,
    lsh, lsh_recv, lsc, lsc_recv, mst, mst_recv, t_acc, t_part, tg_send, tg_recv,
    gr_all, gk_acc, gk_send, gk_recv, gq_f, gq_send, gq_recv, gw_send, gw_recv, ikt, lat_ref,
    q_sem, lg_s, lg_r, lsh_s, lsh_r, lsc_s, lsc_r, mst_s, mst_r, tg_s, tg_r,
    gr_s, gr_r, gk_s, gk_r, gq_s, gq_r, gw_s, gw_r,
):
    rows = latt_ref.shape[1]
    share = rows // nh
    pair = LANES // queries
    blocks = queries * hl // LANES
    jblocks = queries * jl // LANES
    drows = queries * jl // nc
    chunks = blocks // GROUP
    c = lax.axis_index("ctx")
    h = lax.axis_index("head")
    scale2 = LOG2E / math.sqrt(QK_HEAD)
    own = pl.ds(pl.multiple_of(h * share, share), share)
    base = c * rows
    own_base = base + h * share

    load_q = pltpu.make_async_copy(q_hbm, q_buf, q_sem)
    load_q.start()

    barrier = pltpu.get_barrier_semaphore()
    for o in range(1, nc):
        pl.semaphore_signal(barrier, inc=1, device_id={"ctx": lax.rem(c + o, nc)}, device_id_type=MESH)
    for o in range(1, nh):
        pl.semaphore_signal(barrier, inc=1, device_id={"head": lax.rem(h + o, nh)}, device_id_type=MESH)

    lg_part[...] = jnp.zeros_like(lg_part)

    def logit_block(b, carry):
        at = pl.ds(pl.multiple_of(b * LANES, LANES), LANES)
        inner = dot_nt(ik_ref[...], iq_ref[at, :])
        inner_buf[b] = inner
        p = jnp.maximum(inner, 0.0) * w_ref[pl.ds(b, 1), :]
        pick = jnp.where(spread((LANES, queries), 1, jl, b * LANES), 1.0, 0.0).astype(BF16)
        hi = p.astype(BF16)
        rest = p - hi.astype(F32)
        mid = rest.astype(BF16)
        low = (rest - mid.astype(F32)).astype(BF16)
        lg_part[...] += dot(hi, pick) + dot(mid, pick) + dot(low, pick)
        return carry

    lax.fori_loop(0, jblocks, logit_block, 0)
    ikt[...] = ik_ref[...].astype(F32).T.astype(BF16)
    lat_ref[...] = latt_ref[...].T
    limit = jnp.concatenate([pos_ref[...] - base] * pair, axis=1)

    pl.semaphore_wait(barrier, nc - 1 + nh - 1)

    def head_rows(ref):
        return lambda d: ref.at[pl.ds(pl.multiple_of(d * share, share), share), :]

    pending = []
    lg_copies = start_all("head", nh, h, head_rows(lg_part), lambda o: lg_recv.at[o], lg_s, lg_r)
    pending += lg_copies
    load_q.wait()

    def score_chunk(k):
        def score_block(i, carry):
            b = k * GROUP + i
            q = jnp.concatenate([q_buf[b * pair + p] for p in range(pair)], axis=1)
            s = dot(lat_ref[...], q)
            s = jnp.where(iota(s.shape, 0) <= limit, s, MASKED)
            m = jnp.maximum(jnp.max(s, axis=0, keepdims=True), FLOOR)
            e = jnp.exp2((s - m) * scale2)
            e_buf[b] = e.astype(BF16)
            mst[k, pl.ds(i, 1), :] = m
            mst[k, pl.ds(GROUP + i, 1), :] = jnp.sum(e, axis=0, keepdims=True)
            return carry

        lax.fori_loop(0, GROUP, score_block, 0)
        return start_all(
            "ctx", nc, c, lambda d: mst.at[k], lambda o: mst_recv.at[k, o], mst_s.at[k], mst_r.at[k]
        )

    def logit_stats():
        for copy in lg_copies:
            copy.wait_recv()
        total = lg_part[own, :]
        for o in range(1, nh):
            total = total + lg_recv[o]
        total = jnp.where(iota(total.shape, 0) <= pos_ref[...] - own_base, total, MASKED)
        lgq[...] = total
        m = jnp.maximum(jnp.max(total, axis=0, keepdims=True), FLOOR)
        lsh[0:1, :] = m
        lsh[1:2, :] = jnp.sum(jnp.exp2((total - m) * LOG2E), axis=0, keepdims=True)
        return start_all("head", nh, h, lambda d: lsh, lambda o: lsh_recv.at[o], lsh_s, lsh_r)

    def combine(mine, others):
        m = mine[0:1, :]
        for other in others:
            m = jnp.maximum(m, other[0:1, :])
        total = mine[1:2, :] * jnp.exp2((mine[0:1, :] - m) * LOG2E)
        for other in others:
            total = total + other[1:2, :] * jnp.exp2((other[0:1, :] - m) * LOG2E)
        return m, total

    def logit_stats_ctx(copies):
        for copy in copies:
            copy.wait_recv()
        m, total = combine(lsh[...], [lsh_recv[o] for o in range(1, nh)])
        lsc[0:1, :] = m
        lsc[1:2, :] = total
        return start_all("ctx", nc, c, lambda d: lsc, lambda o: lsc_recv.at[o], lsc_s, lsc_r)

    lsh[...] = jnp.zeros_like(lsh)
    lsc[...] = jnp.zeros_like(lsc)
    mst_copies = []
    lsh_copies = lsc_copies = None
    for k in range(chunks):
        mst_copies.append(score_chunk(k))
        if k == min(1, chunks - 1):
            lsh_copies = logit_stats()
        if k == min(2, chunks - 1):
            lsc_copies = logit_stats_ctx(lsh_copies)
    pending += lsh_copies + lsc_copies
    for copies in mst_copies:
        pending += copies

    t_acc[...] = jnp.zeros_like(t_acc)
    same = lax.rem(iota((queries, LANES), 1), queries) == iota((queries, LANES), 0)
    for k in range(chunks):
        for copy in mst_copies[k]:
            copy.wait_recv()
        mine = mst[k]
        highest = mine[:GROUP]
        for o in range(1, nc):
            highest = jnp.maximum(highest, mst_recv[k, o, :GROUP, :])
        shift = jnp.exp2((mine[:GROUP] - highest) * scale2)
        total = mine[GROUP:] * shift
        for o in range(1, nc):
            total = total + mst_recv[k, o, GROUP:, :] * jnp.exp2(
                (mst_recv[k, o, :GROUP, :] - highest) * scale2
            )
        factor = shift / total
        for i in range(GROUP):
            b = k * GROUP + i
            full = jnp.where(same, factor[i : i + 1, :], 0.0)
            hi = full.astype(BF16)
            low = (full - hi.astype(F32)).astype(BF16)
            t_acc[...] += dot_nt(e_buf[b], jnp.concatenate([hi, low], axis=0))
    t_part[...] = t_acc[:, :queries] + t_acc[:, queries:]
    tg_send[...] = t_part[...].astype(BF16)
    tg_copies = start_all("head", nh, h, head_rows(tg_send), lambda o: tg_recv.at[o], tg_s, tg_r)
    pending += tg_copies

    for copy in lsc_copies:
        copy.wait_recv()
    high, total = combine(lsc[...], [lsc_recv[o] for o in range(1, nc)])
    logits = lgq[...]
    predicted = jnp.exp2((logits - high) * LOG2E) * (1.0 / total)
    for copy in tg_copies:
        copy.wait_recv()
    target = t_part[own, :]
    for o in range(1, nh):
        target = target + tg_recv[o].astype(F32)
    gradient = jnp.where(
        iota(target.shape, 0) <= pos_ref[...] - own_base,
        math.sqrt(rows * nc) * (predicted - target * (1.0 / HEADS)),
        0.0,
    )
    gr_all[own, :] = gradient.astype(BF16)
    gr_copies = start_all("head", nh, h, lambda d: gr_all.at[own, :], lambda o: gr_all.at[own, :], gr_s, gr_r)
    pending += gr_copies
    for copy in gr_copies:
        copy.wait_recv()

    gk_acc[...] = jnp.zeros_like(gk_acc)

    def grad_block(b):
        at = pl.ds(pl.multiple_of(b * LANES, LANES), LANES)
        pick = jnp.where(spread((queries, LANES), 0, jl, b * LANES), 1.0, 0.0).astype(BF16)
        grad = dot(gr_all[...], pick)
        inner = inner_buf[b]
        gw_send[pl.ds(b, 1), :] = jnp.sum(grad * jnp.maximum(inner, 0.0), axis=0, keepdims=True)
        delta = jnp.where(inner > 0, grad * w_ref[pl.ds(b, 1), :], 0.0).astype(BF16)
        gk_acc[...] += dot(delta, iq_ref[at, :])
        block = dot(ikt[...], delta).T
        gq_f[at, :] = block
        gq_send[at, :] = block.astype(BF16)

    def gq_copy(o):
        dest = lax.rem(c + o, nc)
        return pltpu.make_async_remote_copy(
            src_ref=gq_send.at[pl.ds(pl.multiple_of(dest * drows, drows), drows), :],
            dst_ref=gq_recv.at[o],
            send_sem=gq_s.at[o],
            recv_sem=gq_r.at[o],
            device_id={"ctx": dest},
            device_id_type=MESH,
        )

    if jblocks == nc:
        def grad_step(o, carry):
            grad_block(lax.rem(c + o, nc))
            gq_copy(o).start()
            return carry

        lax.fori_loop(1, nc, grad_step, 0)
        grad_block(c)
    else:
        def grad_step(b, carry):
            grad_block(b)
            return carry

        lax.fori_loop(0, jblocks, grad_step, 0)
        for o in range(1, nc):
            gq_copy(o).start()
    gk_send[...] = gk_acc[...].astype(BF16)
    gk_copies = start_all("head", nh, h, head_rows(gk_send), lambda o: gk_recv.at[o], gk_s, gk_r)
    gw_copies = start_all("ctx", nc, c, lambda d: gw_send, lambda o: gw_recv.at[o], gw_s, gw_r)
    gq_copies = [gq_copy(o) for o in range(1, nc)]
    pending += gk_copies + gw_copies + gq_copies

    for copy in gk_copies:
        copy.wait_recv()
    total = gk_acc[own, :]
    for o in range(1, nh):
        total = total + gk_recv[o].astype(F32)
    gk_out[...] = total
    for copy in gq_copies:
        copy.wait_recv()
    total = gq_f[pl.ds(pl.multiple_of(c * drows, drows), drows), :]
    for o in range(1, nc):
        total = total + gq_recv[o].astype(F32)
    gq_out[...] = total
    for copy in gw_copies:
        copy.wait_recv()
    total = gw_send[...]
    for o in range(1, nc):
        total = total + gw_recv[o]
    gw_out[...] = total
    for copy in pending:
        copy.wait_send()


def local(nc, nh, positions, mla_queries, latent_keys, index_queries, index_keys, head_weights):
    queries, hl, dqk = mla_queries.shape
    _, jl, di = index_queries.shape
    rows = latent_keys.shape[0]
    share = rows // nh
    blocks = queries * hl // LANES
    jblocks = queries * jl // LANES
    chunks = blocks // GROUP
    own = queries // nc
    drows = own * jl
    q = mla_queries.transpose(1, 2, 0)
    iq = index_queries.reshape(queries * jl, di)
    w = head_weights.reshape(jblocks, LANES)
    vm = pltpu.VMEM
    dma = pltpu.SemaphoreType.DMA
    vspec = pl.BlockSpec(memory_space=pltpu.VMEM)
    gq, gk, gw = pl.pallas_call(
        functools.partial(kernel, nc, nh, hl, jl, queries),
        out_shape=(
            jax.ShapeDtypeStruct((drows, di), F32),
            jax.ShapeDtypeStruct((share, di), F32),
            jax.ShapeDtypeStruct((jblocks, LANES), F32),
        ),
        in_specs=[pl.BlockSpec(memory_space=pl.ANY)] + [vspec] * 5,
        out_specs=(vspec, vspec, vspec),
        scratch_shapes=[
            vm((hl, dqk, queries), BF16),
            vm((blocks, rows, LANES), BF16),
            vm((jblocks, rows, LANES), F32),
            vm((rows, queries), F32),
            vm((nh, share, queries), F32),
            vm((share, queries), F32),
            vm((8, queries), F32),
            vm((nh, 8, queries), F32),
            vm((8, queries), F32),
            vm((nc, 8, queries), F32),
            vm((chunks, 2 * GROUP, LANES), F32),
            vm((chunks, nc, 2 * GROUP, LANES), F32),
            vm((rows, 2 * queries), F32),
            vm((rows, queries), F32),
            vm((rows, queries), BF16),
            vm((nh, share, queries), BF16),
            vm((rows, queries), BF16),
            vm((rows, di), F32),
            vm((rows, di), BF16),
            vm((nh, share, di), BF16),
            vm((queries * jl, di), F32),
            vm((queries * jl, di), BF16),
            vm((nc, drows, di), BF16),
            vm((jblocks, LANES), F32),
            vm((nc, jblocks, LANES), F32),
            vm((di, rows), BF16),
            vm((rows, dqk), BF16),
            dma,
            dma((nh,)), dma((nh,)),
            dma((nh,)), dma((nh,)),
            dma((nc,)), dma((nc,)),
            dma((chunks, nc)), dma((chunks, nc)),
            dma((nh,)), dma((nh,)),
            dma((nh,)), dma((nh,)),
            dma((nh,)), dma((nh,)),
            dma((nc,)), dma((nc,)),
            dma((nc,)), dma((nc,)),
        ],
        compiler_params=pltpu.CompilerParams(
            collective_id=0, has_side_effects=True, vmem_limit_bytes=60 * 1024 * 1024
        ),
    )(q, latent_keys.T, iq, index_keys, w, positions.reshape(1, queries))
    gw = lax.dynamic_slice_in_dim(gw.reshape(queries, jl), lax.axis_index("ctx") * own, own, 0)
    return gq.reshape(own, jl, di), gk, gw


def solution(mesh):
    in_specs = (
        P(),
        P(None, "head", None),
        P("ctx", None),
        P(None, "head", None),
        P("ctx", None),
        P(None, "head"),
    )
    out_specs = (P("ctx", "head", None), P(("ctx", "head"), None), P("ctx", "head"))
    body = functools.partial(local, mesh.shape["ctx"], mesh.shape["head"])
    return jax.shard_map(body, mesh=mesh, in_specs=in_specs, out_specs=out_specs, check_vma=False)
```

time: 319 us -> 66.1 us (0.21)
  waiting for transfers between devices: 160 us -> 0 us
  blocking collectives: 75.9 us -> 0 us
  Pallas kernels: 0 us -> 59.2 us
  matrix products: 41.3 us -> 0 us
  other arithmetic: 24.2 us -> 0 us
  between operations: 13.9 us -> 0.65 us
    reduce_scatter x5 -> x0, waiting for transfers between devices: 160 us -> none  [the longest x1 63.7 us: local(): lax.psum_scatter(weight_part, 'ctx', scatter_dimension=0, tiled=True)]
    pallas_call x0 -> x1, Pallas kernels: none -> 59.2 us  [local(): pl.pallas_call(functools.partial(kernel, nc, nh, hl, jl, queries), out_sh...]
    dot_general x5 -> x0, matrix products: 41.3 us -> none  [the longest x1 13.6 us: local(): jnp.einsum('ts,tjs->tj', grad_float, active, precision=lax.Precision.HIGH...]
    pmax x1 -> x0, blocking collectives: 37.1 us -> none  [local(): highest = lax.pmax(masked_highest(scores, head_mask), 'ctx')]
    psum x1 -> x0, blocking collectives: 33 us -> none  [local(): totals = lax.psum(jnp.sum(exponent, axis=-1), 'ctx')]
    reduce_sum x3 -> x0, other arithmetic: 17.3 us -> none  [the longest x1 9.14 us: local(): totals = lax.psum(jnp.sum(exponent, axis=-1), 'ctx')]
    all_gather x1 -> x0, blocking collectives: 5.78 us -> none  [local(): gradient = lax.all_gather(gradient, 'head', axis=0, tiled=True)]
    unnamed x1 -> x0, other arithmetic: 4.62 us -> none
  transfers between devices with their start and end apart: 5 -> 0, of which waited for: 5 -> 0; matrix products, arithmetic and copies ran while one was open for 11% -> 0% of each run, Pallas kernels for 0% -> 0%
where the time goes in v1:
time: 66.1 us; the launch traced here: 65.8 us
  Pallas kernels  59.2 us (90%)
  local copies, waits for them, and re-layouts  6 us (9%)
    pallas_call x1, Pallas kernels, local(): pl.pallas_call(functools.partial(kernel, nc, nh, hl, jl, queries), out_sh...  59.2 us
    unnamed x3, local copies, waits for them, and re-layouts  3.93 us

profile of v1, /device:TPU:0, one launch (start us, length us, event | category | flops | bytes accessed | tf_op | source)
XLA Modules:
  0.0 65.8 jit_solution(4250655414493300410)
XLA Ops:
  0.6 0.8 %copy.10 = f32[128,16]{1,0:T(8,128)S(1)} copy(f32[128,16]{0,1:T(8,128)} %param.11) | data formatting | bytes 16384 | tf_op args[5]
  1.4 0.7 %reshape.22.w_ref = f32[8,256]{1,0:T(8,128)} reshape(f32[128,16]{1,0:T(8,128)S(1)} %copy.10) | data formatting | bytes 16384 | tf_op jit(solution)/shard_map/reshape | solution.py:313
  2.1 59.2 %shard_map.85 = (f32[256,128]{1,0:T(8,128)}, f32[256,128]{1,0:T(8,128)}, f32[8,256]{1,0:T(8,128)}) custom-call(bf16[32,576,128]{2,1,0:T(8,128)(2,1)} %bitcast.5, bf16[576,1024]{1,0:T(8,128)(2,1)} %bitcast.6, bf16[2048,128]{1,0:T(8,128)(2,1)} %bitcast.7, bf16[1024,128]{1,0:T(8,128)(2,1)} %ik_ref.1, f32[8,256]{1,0:T(8,128)} %reshape.22.w_ref, s32[1,128]{1,0:T(1,128)} %bitcast.9), custom_call_target="tpu_custom_call" | custom-call | tf_op jit(solution)/shard_map/pallas_call | solution.py:317
  61.3 0.8 %reshape.25 = f32[128,16]{1,0:T(8,128)S(1)} reshape(f32[8,256]{1,0:T(8,128)} %get-tuple-element.8) | data formatting | bytes 16384 | tf_op jit(solution)/shard_map/reshape | solution.py:369
  62.1 0.6 constant_dynamic-slice_fusion
  62.7 1.6 %copy.13 = f32[16,16,128]{2,1,0:T(8,128)} copy(f32[16,16,128]{2,1,0:T(8,128)} %bitcast.8) | data formatting | bytes 262144
  64.3 1.6 %copy.14 = f32[256,128]{1,0:T(8,128)} copy(f32[256,128]{1,0:T(8,128)} %get-tuple-element.13) | data formatting | bytes 262144

commit v2 on v1

--- a/solution.py
+++ b/solution.py
@@ -37,6 +37,13 @@
     query = iota(shape, query_dim) * width
     lane = iota(shape, 1 - query_dim) + first
     return (query <= lane) & (lane < query + width)
+
+
+def terms(x):
+    hi = x.astype(BF16)
+    rest = x - hi.astype(F32)
+    mid = rest.astype(BF16)
+    return hi, mid, (rest - mid.astype(F32)).astype(BF16)
 
 
 def start_all(axis, n, me, source, slot, send, recv):
@@ -58,11 +65,11 @@
 
 def kernel(
     nc, nh, hl, jl, queries,
-    q_hbm, latt_ref, iq_ref, ik_ref, w_ref, pos_ref,
+    q_hbm, latt_ref, iq_ref, ik_ref, wt_ref, pos_ref,
     gq_out, gk_out, gw_out,
     q_buf, e_buf, inner_buf, lg_part, lg_recv, lgq,
     lsh, lsh_recv, lsc, lsc_recv, mst, mst_recv, t_acc, t_part, tg_send, tg_recv,
-    gr_all, gk_acc, gk_send, gk_recv, gq_f, gq_send, gq_recv, gw_send, gw_recv, ikt, lat_ref,
+    gr_all, gk_acc, gk_send, gk_recv, gq_f, gq_send, gq_recv, gw_send, gw_recv, ikt, lat_ref, w_ref, s_even, s_odd,
     q_sem, lg_s, lg_r, lsh_s, lsh_r, lsc_s, lsc_r, mst_s, mst_r, tg_s, tg_r,
     gr_s, gr_r, gk_s, gk_r, gq_s, gq_r, gw_s, gw_r,
 ):
@@ -95,13 +102,15 @@
         at = pl.ds(pl.multiple_of(b * LANES, LANES), LANES)
         inner = dot_nt(ik_ref[...], iq_ref[at, :])
         inner_buf[b] = inner
-        p = jnp.maximum(inner, 0.0) * w_ref[pl.ds(b, 1), :]
+        across = jnp.where(spread((queries, LANES), 0, jl, b * LANES), 1.0, 0.0).astype(BF16)
+        weights = sum(dot(term, across) for term in terms(wt_ref[...]))
+        head = lax.rem(iota((jl, LANES), 1), jl)
+        weights = jnp.where(head == iota((jl, LANES), 0), weights, 0.0)
+        weights = jnp.sum(weights, axis=0, keepdims=True)
+        w_ref[pl.ds(b, 1), :] = weights
+        p = jnp.maximum(inner, 0.0) * weights
         pick = jnp.where(spread((LANES, queries), 1, jl, b * LANES), 1.0, 0.0).astype(BF16)
-        hi = p.astype(BF16)
-        rest = p - hi.astype(F32)
-        mid = rest.astype(BF16)
-        low = (rest - mid.astype(F32)).astype(BF16)
-        lg_part[...] += dot(hi, pick) + dot(mid, pick) + dot(low, pick)
+        lg_part[...] += dot(jnp.concatenate(terms(p), axis=1), jnp.concatenate([pick] * 3, axis=0))
         return carry
 
     lax.fori_loop(0, jblocks, logit_block, 0)
@@ -119,20 +128,32 @@
     pending += lg_copies
     load_q.wait()
 
-    def score_chunk(k):
-        def score_block(i, carry):
-            b = k * GROUP + i
-            q = jnp.concatenate([q_buf[b * pair + p] for p in range(pair)], axis=1)
-            s = dot(lat_ref[...], q)
-            s = jnp.where(iota(s.shape, 0) <= limit, s, MASKED)
-            m = jnp.maximum(jnp.max(s, axis=0, keepdims=True), FLOOR)
-            e = jnp.exp2((s - m) * scale2)
-            e_buf[b] = e.astype(BF16)
-            mst[k, pl.ds(i, 1), :] = m
-            mst[k, pl.ds(GROUP + i, 1), :] = jnp.sum(e, axis=0, keepdims=True)
-            return carry
-
-        lax.fori_loop(0, GROUP, score_block, 0)
+    def scores(b, out):
+        q = jnp.concatenate([q_buf[b * pair + p] for p in range(pair)], axis=1)
+        s = dot(lat_ref[...], q)
+        s = jnp.where(iota(s.shape, 0) <= limit, s, MASKED)
+        out[...] = s
+        return jnp.maximum(jnp.max(s, axis=0, keepdims=True), FLOOR)
+
+    def exponentials(k, i, src, m):
+        e = jnp.exp2((src[...] - m) * scale2)
+        e_buf[k * GROUP + i] = e.astype(BF16)
+        mst[k, pl.ds(i, 1), :] = m
+        mst[k, pl.ds(GROUP + i, 1), :] = jnp.sum(e, axis=0, keepdims=True)
+
+    def score_chunk(k, m):
+        def score_pair(j, m):
+            b = k * GROUP + 2 * j
+            m_odd = scores(b + 1, s_odd)
+            exponentials(k, 2 * j, s_even, m)
+            m_even = scores(lax.rem(b + 2, blocks), s_even)
+            exponentials(k, 2 * j + 1, s_odd, m_odd)
+            return m_even
+
+        m = lax.fori_loop(0, GROUP // 2, score_pair, m)
+        return m, score_send(k)
+
+    def score_send(k):
         return start_all(
             "ctx", nc, c, lambda d: mst.at[k], lambda o: mst_recv.at[k, o], mst_s.at[k], mst_r.at[k]
         )
@@ -170,9 +191,11 @@
     lsh[...] = jnp.zeros_like(lsh)
     lsc[...] = jnp.zeros_like(lsc)
     mst_copies = []
+    high = scores(0, s_even)
     lsh_copies = lsc_copies = None
     for k in range(chunks):
-        mst_copies.append(score_chunk(k))
+        high, copies = score_chunk(k, high)
+        mst_copies.append(copies)
         if k == min(1, chunks - 1):
             lsh_copies = logit_stats()
         if k == min(2, chunks - 1):
@@ -293,9 +316,21 @@
     total = gw_send[...]
     for o in range(1, nc):
         total = total + gw_recv[o]
-    gw_out[...] = total
+    picked = jnp.zeros((queries // nc, LANES), F32)
+    for b in range(jblocks):
+        mine = spread(picked.shape, 0, jl, b * LANES - c * drows)
+        picked = picked + jnp.where(mine, total[b : b + 1, :], 0.0)
+    head = lax.rem(iota((LANES, jl), 0), jl) == iota((LANES, jl), 1)
+    head = jnp.where(head, 1.0, 0.0).astype(BF16)
+    gw_out[...] = sum(dot(term, head) for term in terms(picked))
     for copy in pending:
         copy.wait_send()
+
+
+def finish(a_ref, b_ref, c_ref, a_out, b_out, c_out):
+    a_out[...] = a_ref[...]
+    b_out[...] = b_ref[...]
+    c_out[...] = c_ref[...]
 
 
 def local(nc, nh, positions, mla_queries, latent_keys, index_queries, index_keys, head_weights):
@@ -310,7 +345,6 @@
     drows = own * jl
     q = mla_queries.transpose(1, 2, 0)
     iq = index_queries.reshape(queries * jl, di)
-    w = head_weights.reshape(jblocks, LANES)
     vm = pltpu.VMEM
     dma = pltpu.SemaphoreType.DMA
     vspec = pl.BlockSpec(memory_space=pltpu.VMEM)
@@ -319,7 +353,7 @@
         out_shape=(
             jax.ShapeDtypeStruct((drows, di), F32),
             jax.ShapeDtypeStruct((share, di), F32),
-            jax.ShapeDtypeStruct((jblocks, LANES), F32),
+            jax.ShapeDtypeStruct((own, jl), F32),
         ),
         in_specs=[pl.BlockSpec(memory_space=pl.ANY)] + [vspec] * 5,
         out_specs=(vspec, vspec, vspec),
@@ -351,6 +385,9 @@
             vm((nc, jblocks, LANES), F32),
             vm((di, rows), BF16),
             vm((rows, dqk), BF16),
+            vm((jblocks, LANES), F32),
+            vm((rows, LANES), F32),
+            vm((rows, LANES), F32),
             dma,
             dma((nh,)), dma((nh,)),
             dma((nh,)), dma((nh,)),
@@ -365,8 +402,13 @@
         compiler_params=pltpu.CompilerParams(
             collective_id=0, has_side_effects=True, vmem_limit_bytes=60 * 1024 * 1024
         ),
-    )(q, latent_keys.T, iq, index_keys, w, positions.reshape(1, queries))
-    gw = lax.dynamic_slice_in_dim(gw.reshape(queries, jl), lax.axis_index("ctx") * own, own, 0)
+    )(q, latent_keys.T, iq, index_keys, head_weights.T, positions.reshape(1, queries))
+    gq, gk, gw = pl.pallas_call(
+        finish,
+        out_shape=tuple(jax.ShapeDtypeStruct(x.shape, F32) for x in (gq, gk, gw)),
+        in_specs=[vspec] * 3,
+        out_specs=(vspec,) * 3,
+    )(gq, gk, gw)
     return gq.reshape(own, jl, di), gk, gw
 
 

time: 66.1 us -> 59.4 us (0.90)
  local copies, waits for them, and re-layouts: 6 us -> 0 us
    unnamed x3 -> x0, local copies, waits for them, and re-layouts: 3.93 us -> none
    pallas_call x1, Pallas kernels: 59.2 us -> 57 us  [local(): pl.pallas_call(functools.partial(kernel, nc, nh, hl, jl, queries), out_sh...]
    pallas_call x0 -> x1, Pallas kernels: none -> 1.68 us  [local(): pl.pallas_call(finish, out_shape=tuple((jax.ShapeDtypeStruct(x.shape, F32...]
    reshape x2 -> x0, local copies, waits for them, and re-layouts: 1.46 us -> none  [the longest x1 0.77 us: local(): gw.reshape(queries, jl)]
where the time goes in v2:
time: 59.4 us; the launch traced here: 59.3 us
  Pallas kernels  58.6 us (99%)
  between operations  0.64 us (1%)
    pallas_call x1, Pallas kernels, local(): pl.pallas_call(functools.partial(kernel, nc, nh, hl, jl, queries), out_sh...  57 us
    pallas_call x1, Pallas kernels, local(): pl.pallas_call(finish, out_shape=tuple((jax.ShapeDtypeStruct(x.shape, F32...  1.68 us

profile of v2, /device:TPU:0, one launch (start us, length us, event | category | flops | bytes accessed | tf_op | source)
XLA Modules:
  0.0 59.3 jit_solution(14946587627637748379)
XLA Ops:
  0.6 57.0 %shard_map.85 = (f32[256,128]{1,0:T(8,128)}, f32[256,128]{1,0:T(8,128)}, f32[16,16]{1,0:T(8,128)}) custom-call(bf16[32,576,128]{2,1,0:T(8,128)(2,1)} %bitcast.6, bf16[576,1024]{1,0:T(8,128)(2,1)} %bitcast.7, bf16[2048,128]{1,0:T(8,128)(2,1)} %bitcast.8, bf16[1024,128]{1,0:T(8,128)(2,1)} %ik_ref.1, f32[16,128]{1,0:T(8,128)} %bitcast.9, s32[1,128]{1,0:T(1,128)} %bitcast.10), custom_call_target="tpu_custom_call" | custom-call | tf_op jit(solution)/shard_map/pallas_call | solution.py:351
  57.6 1.7 %shard_map.86 = (f32[256,128]{1,0:T(8,128)}, f32[256,128]{1,0:T(8,128)}, f32[16,16]{1,0:T(8,128)}) custom-call(f32[256,128]{1,0:T(8,128)} %get-tuple-element.9.a_ref, f32[256,128]{1,0:T(8,128)} %get-tuple-element.10.b_ref, f32[16,16]{1,0:T(8,128)} %get-tuple-element.11.c_ref), custom_call_target="tpu_custom_call" | custom-call | tf_op jit(solution)/shard_map/pallas_call | solution.py:406

commit v3 on v2

--- a/solution.py
+++ b/solution.py
@@ -192,15 +192,11 @@
     lsc[...] = jnp.zeros_like(lsc)
     mst_copies = []
     high = scores(0, s_even)
-    lsh_copies = lsc_copies = None
     for k in range(chunks):
         high, copies = score_chunk(k, high)
         mst_copies.append(copies)
-        if k == min(1, chunks - 1):
-            lsh_copies = logit_stats()
-        if k == min(2, chunks - 1):
-            lsc_copies = logit_stats_ctx(lsh_copies)
-    pending += lsh_copies + lsc_copies
+    lsh_copies = logit_stats()
+    pending += lsh_copies
     for copies in mst_copies:
         pending += copies
 
@@ -226,6 +222,9 @@
             hi = full.astype(BF16)
             low = (full - hi.astype(F32)).astype(BF16)
             t_acc[...] += dot_nt(e_buf[b], jnp.concatenate([hi, low], axis=0))
+        if k == (chunks - 1) // 2:
+            lsc_copies = logit_stats_ctx(lsh_copies)
+            pending += lsc_copies
     t_part[...] = t_acc[:, :queries] + t_acc[:, queries:]
     tg_send[...] = t_part[...].astype(BF16)
     tg_copies = start_all("head", nh, h, head_rows(tg_send), lambda o: tg_recv.at[o], tg_s, tg_r)

time: 59.4 us -> 58.5 us (0.985)
  Pallas kernels: 58.6 us -> 57.7 us
    pallas_call x1, Pallas kernels: 57 us -> 56 us  [local(): pl.pallas_call(functools.partial(kernel, nc, nh, hl, jl, queries), out_sh...]
where the time goes in v3:
time: 58.5 us; the launch traced here: 58.3 us
  Pallas kernels  57.7 us (99%)
  between operations  0.64 us (1%)
    pallas_call x1, Pallas kernels, local(): pl.pallas_call(functools.partial(kernel, nc, nh, hl, jl, queries), out_sh...  56 us
    pallas_call x1, Pallas kernels, local(): pl.pallas_call(finish, out_shape=tuple((jax.ShapeDtypeStruct(x.shape, F32...  1.68 us

profile of v3, /device:TPU:0, one launch (start us, length us, event | category | flops | bytes accessed | tf_op | source)
XLA Modules:
  0.0 58.3 jit_solution(17464700622415997425)
XLA Ops:
  0.6 56.0 %shard_map.85 = (f32[256,128]{1,0:T(8,128)}, f32[256,128]{1,0:T(8,128)}, f32[16,16]{1,0:T(8,128)}) custom-call(bf16[32,576,128]{2,1,0:T(8,128)(2,1)} %bitcast.6, bf16[576,1024]{1,0:T(8,128)(2,1)} %bitcast.7, bf16[2048,128]{1,0:T(8,128)(2,1)} %bitcast.8, bf16[1024,128]{1,0:T(8,128)(2,1)} %ik_ref.1, f32[16,128]{1,0:T(8,128)} %bitcast.9, s32[1,128]{1,0:T(1,128)} %bitcast.10), custom_call_target="tpu_custom_call" | custom-call | tf_op jit(solution)/shard_map/pallas_call | solution.py:350
  56.6 1.7 %shard_map.86 = (f32[256,128]{1,0:T(8,128)}, f32[256,128]{1,0:T(8,128)}, f32[16,16]{1,0:T(8,128)}) custom-call(f32[256,128]{1,0:T(8,128)} %get-tuple-element.9.a_ref, f32[256,128]{1,0:T(8,128)} %get-tuple-element.10.b_ref, f32[16,16]{1,0:T(8,128)} %get-tuple-element.11.c_ref), custom_call_target="tpu_custom_call" | custom-call | tf_op jit(solution)/shard_map/pallas_call | solution.py:405

commit v4 on v3

--- a/solution.py
+++ b/solution.py
@@ -69,9 +69,9 @@
     gq_out, gk_out, gw_out,
     q_buf, e_buf, inner_buf, lg_part, lg_recv, lgq,
     lsh, lsh_recv, lsc, lsc_recv, mst, mst_recv, t_acc, t_part, tg_send, tg_recv,
-    gr_all, gk_acc, gk_send, gk_recv, gq_f, gq_send, gq_recv, gw_send, gw_recv, ikt, lat_ref, w_ref, s_even, s_odd,
+    gr_all, gk_acc, gk_send, gk_recv, gq_f, gq_send, gq_recv, gw_send, gw_recv, ikt, lat_ref, w_ref, s_even, s_odd, pair_recv, gq_sum,
     q_sem, lg_s, lg_r, lsh_s, lsh_r, lsc_s, lsc_r, mst_s, mst_r, tg_s, tg_r,
-    gr_s, gr_r, gk_s, gk_r, gq_s, gq_r, gw_s, gw_r,
+    gr_s, gr_r, gk_s, gk_r, gq_s, gq_r, gw_s, gw_r, pair_s, pair_r,
 ):
     rows = latt_ref.shape[1]
     share = rows // nh
@@ -265,10 +265,24 @@
         gq_f[at, :] = block
         gq_send[at, :] = block.astype(BF16)
 
+    def gq_rows(dest):
+        return pl.ds(pl.multiple_of(dest * drows, drows), drows)
+
+    def pair_copy(o):
+        dest = lax.rem(c // 2 + o, half) * 2 + 1 - lax.rem(c, 2)
+        return pltpu.make_async_remote_copy(
+            src_ref=gq_send.at[gq_rows(dest), :],
+            dst_ref=pair_recv.at[o],
+            send_sem=pair_s.at[o],
+            recv_sem=pair_r.at[o],
+            device_id={"ctx": c + 1 - 2 * lax.rem(c, 2)},
+            device_id_type=MESH,
+        )
+
     def gq_copy(o):
-        dest = lax.rem(c + o, nc)
+        dest = lax.rem(c // 2 + o, half) * 2 + lax.rem(c, 2)
         return pltpu.make_async_remote_copy(
-            src_ref=gq_send.at[pl.ds(pl.multiple_of(dest * drows, drows), drows), :],
+            src_ref=gq_sum.at[o],
             dst_ref=gq_recv.at[o],
             send_sem=gq_s.at[o],
             recv_sem=gq_r.at[o],
@@ -276,26 +290,44 @@
             device_id_type=MESH,
         )
 
+    half = nc // 2
+    low = lax.rem(c, 2)
     if jblocks == nc:
-        def grad_step(o, carry):
-            grad_block(lax.rem(c + o, nc))
-            gq_copy(o).start()
+        def grad_away(i, carry):
+            o = lax.rem(i + 1, half)
+            grad_block(lax.rem(c // 2 + o, half) * 2 + 1 - low)
+            pair_copy(o).start()
             return carry
 
-        lax.fori_loop(1, nc, grad_step, 0)
-        grad_block(c)
+        def grad_near(i, carry):
+            grad_block(lax.rem(c // 2 + i + 1, half) * 2 + low)
+            return carry
+
+        lax.fori_loop(0, half, grad_away, 0)
+        lax.fori_loop(0, half, grad_near, 0)
     else:
         def grad_step(b, carry):
             grad_block(b)
             return carry
 
         lax.fori_loop(0, jblocks, grad_step, 0)
-        for o in range(1, nc):
-            gq_copy(o).start()
+        for i in range(half):
+            pair_copy((i + 1) % half).start()
     gk_send[...] = gk_acc[...].astype(BF16)
     gk_copies = start_all("head", nh, h, head_rows(gk_send), lambda o: gk_recv.at[o], gk_s, gk_r)
     gw_copies = start_all("ctx", nc, c, lambda d: gw_send, lambda o: gw_recv.at[o], gw_s, gw_r)
-    gq_copies = [gq_copy(o) for o in range(1, nc)]
+    pair_copies = [pair_copy(o) for o in range(half)]
+    gq_copies = [gq_copy(o) for o in range(1, half)]
+
+    def pair_sum(o):
+        pair_copies[o].wait_recv()
+        dest = lax.rem(c // 2 + o, half) * 2 + low
+        return gq_f[gq_rows(dest), :] + pair_recv[o].astype(F32)
+
+    for o in range(1, half):
+        gq_sum[o] = pair_sum(o).astype(BF16)
+        gq_copies[o - 1].start()
+    pending += pair_copies
     pending += gk_copies + gw_copies + gq_copies
 
     for copy in gk_copies:
@@ -304,10 +336,9 @@
     for o in range(1, nh):
         total = total + gk_recv[o].astype(F32)
     gk_out[...] = total
-    for copy in gq_copies:
-        copy.wait_recv()
-    total = gq_f[pl.ds(pl.multiple_of(c * drows, drows), drows), :]
-    for o in range(1, nc):
+    total = pair_sum(0)
+    for o in range(1, half):
+        gq_copies[o - 1].wait_recv()
         total = total + gq_recv[o].astype(F32)
     gq_out[...] = total
     for copy in gw_copies:
@@ -379,7 +410,7 @@
             vm((nh, share, di), BF16),
             vm((queries * jl, di), F32),
             vm((queries * jl, di), BF16),
-            vm((nc, drows, di), BF16),
+            vm((nc // 2, drows, di), BF16),
             vm((jblocks, LANES), F32),
             vm((nc, jblocks, LANES), F32),
             vm((di, rows), BF16),
@@ -387,6 +418,8 @@
             vm((jblocks, LANES), F32),
             vm((rows, LANES), F32),
             vm((rows, LANES), F32),
+            vm((nc // 2, drows, di), BF16),
+            vm((nc // 2, drows, di), BF16),
             dma,
             dma((nh,)), dma((nh,)),
             dma((nh,)), dma((nh,)),
@@ -397,6 +430,7 @@
             dma((nh,)), dma((nh,)),
             dma((nc,)), dma((nc,)),
             dma((nc,)), dma((nc,)),
+            dma((nc // 2,)), dma((nc // 2,)),
         ],
         compiler_params=pltpu.CompilerParams(
             collective_id=0, has_side_effects=True, vmem_limit_bytes=60 * 1024 * 1024

time: 58.5 us -> 54.6 us (0.933)
  Pallas kernels: 57.7 us -> 53.8 us
    pallas_call x1, Pallas kernels: 56 us -> 52.1 us  [local(): pl.pallas_call(functools.partial(kernel, nc, nh, hl, jl, queries), out_sh...]
where the time goes in v4:
time: 54.6 us; the launch traced here: 54.4 us
  Pallas kernels  53.8 us (99%)
  between operations  0.64 us (1%)
    pallas_call x1, Pallas kernels, local(): pl.pallas_call(functools.partial(kernel, nc, nh, hl, jl, queries), out_sh...  52.1 us
    pallas_call x1, Pallas kernels, local(): pl.pallas_call(finish, out_shape=tuple((jax.ShapeDtypeStruct(x.shape, F32...  1.68 us

profile of v4, /device:TPU:0, one launch (start us, length us, event | category | flops | bytes accessed | tf_op | source)
XLA Modules:
  0.0 54.4 jit_solution(5669017652980990933)
XLA Ops:
  0.6 52.1 %shard_map.85 = (f32[256,128]{1,0:T(8,128)}, f32[256,128]{1,0:T(8,128)}, f32[16,16]{1,0:T(8,128)}) custom-call(bf16[32,576,128]{2,1,0:T(8,128)(2,1)} %bitcast.6, bf16[576,1024]{1,0:T(8,128)(2,1)} %bitcast.7, bf16[2048,128]{1,0:T(8,128)(2,1)} %bitcast.8, bf16[1024,128]{1,0:T(8,128)(2,1)} %ik_ref.1, f32[16,128]{1,0:T(8,128)} %bitcast.9, s32[1,128]{1,0:T(1,128)} %bitcast.10), custom_call_target="tpu_custom_call" | custom-call | tf_op jit(solution)/shard_map/pallas_call | solution.py:381
  52.7 1.7 %shard_map.86 = (f32[256,128]{1,0:T(8,128)}, f32[256,128]{1,0:T(8,128)}, f32[16,16]{1,0:T(8,128)}) custom-call(f32[256,128]{1,0:T(8,128)} %get-tuple-element.9.a_ref, f32[256,128]{1,0:T(8,128)} %get-tuple-element.10.b_ref, f32[16,16]{1,0:T(8,128)} %get-tuple-element.11.c_ref), custom_call_target="tpu_custom_call" | custom-call | tf_op jit(solution)/shard_map/pallas_call | solution.py:439

commit v5 on v4

--- a/solution.py
+++ b/solution.py
@@ -65,11 +65,11 @@
 
 def kernel(
     nc, nh, hl, jl, queries,
-    q_hbm, latt_ref, iq_ref, ik_ref, wt_ref, pos_ref,
+    q_hbm, latt_hbm, iq_ref, ik_ref, wt_ref, pos_ref,
     gq_out, gk_out, gw_out,
     q_buf, e_buf, inner_buf, lg_part, lg_recv, lgq,
     lsh, lsh_recv, lsc, lsc_recv, mst, mst_recv, t_acc, t_part, tg_send, tg_recv,
-    gr_all, gk_acc, gk_send, gk_recv, gq_f, gq_send, gq_recv, gw_send, gw_recv, ikt, lat_ref, w_ref, s_even, s_odd, pair_recv, gq_sum,
+    gr_all, gk_acc, gk_send, gk_recv, gq_f, gq_send, gq_recv, gw_send, gw_recv, ikt, lat_ref, w_ref, s_even, s_odd, pair_recv, gq_sum, latt_ref, latt_sem,
     q_sem, lg_s, lg_r, lsh_s, lsh_r, lsc_s, lsc_r, mst_s, mst_r, tg_s, tg_r,
     gr_s, gr_r, gk_s, gk_r, gq_s, gq_r, gw_s, gw_r, pair_s, pair_r,
 ):
@@ -88,6 +88,8 @@
     own_base = base + h * share
 
     load_q = pltpu.make_async_copy(q_hbm, q_buf, q_sem)
+    load_lat = pltpu.make_async_copy(latt_hbm, latt_ref, latt_sem)
+    load_lat.start()
     load_q.start()
 
     barrier = pltpu.get_barrier_semaphore()
@@ -114,8 +116,6 @@
         return carry
 
     lax.fori_loop(0, jblocks, logit_block, 0)
-    ikt[...] = ik_ref[...].astype(F32).T.astype(BF16)
-    lat_ref[...] = latt_ref[...].T
     limit = jnp.concatenate([pos_ref[...] - base] * pair, axis=1)
 
     pl.semaphore_wait(barrier, nc - 1 + nh - 1)
@@ -126,6 +126,9 @@
     pending = []
     lg_copies = start_all("head", nh, h, head_rows(lg_part), lambda o: lg_recv.at[o], lg_s, lg_r)
     pending += lg_copies
+    load_lat.wait()
+    lat_ref[...] = latt_ref[...].T
+    ikt[...] = ik_ref[...].astype(F32).T.astype(BF16)
     load_q.wait()
 
     def scores(b, out):
@@ -385,7 +388,7 @@
             jax.ShapeDtypeStruct((share, di), F32),
             jax.ShapeDtypeStruct((own, jl), F32),
         ),
-        in_specs=[pl.BlockSpec(memory_space=pl.ANY)] + [vspec] * 5,
+        in_specs=[pl.BlockSpec(memory_space=pl.ANY)] * 2 + [vspec] * 4,
         out_specs=(vspec, vspec, vspec),
         scratch_shapes=[
             vm((hl, dqk, queries), BF16),
@@ -420,6 +423,8 @@
             vm((rows, LANES), F32),
             vm((nc // 2, drows, di), BF16),
             vm((nc // 2, drows, di), BF16),
+            vm((dqk, rows), BF16),
+            dma,
             dma,
             dma((nh,)), dma((nh,)),
             dma((nh,)), dma((nh,)),

time: 54.6 us -> 54.2 us (level)
  no operation moved by 1% of the time
where the time goes in v5:
time: 54.2 us; the launch traced here: 54 us
  Pallas kernels  53.4 us (99%)
  between operations  0.64 us (1%)
    pallas_call x1, Pallas kernels, local(): pl.pallas_call(functools.partial(kernel, nc, nh, hl, jl, queries), out_sh...  51.7 us
    pallas_call x1, Pallas kernels, local(): pl.pallas_call(finish, out_shape=tuple((jax.ShapeDtypeStruct(x.shape, F32...  1.68 us

profile of v5, /device:TPU:0, one launch (start us, length us, event | category | flops | bytes accessed | tf_op | source)
XLA Modules:
  0.0 54.0 jit_solution(11612412225088330595)
XLA Ops:
  0.6 51.7 %shard_map.85 = (f32[256,128]{1,0:T(8,128)}, f32[256,128]{1,0:T(8,128)}, f32[16,16]{1,0:T(8,128)}) custom-call(bf16[32,576,128]{2,1,0:T(8,128)(2,1)} %bitcast.6, bf16[576,1024]{1,0:T(8,128)(2,1)} %bitcast.7, bf16[2048,128]{1,0:T(8,128)(2,1)} %bitcast.8, bf16[1024,128]{1,0:T(8,128)(2,1)} %ik_ref.1, f32[16,128]{1,0:T(8,128)} %bitcast.9, s32[1,128]{1,0:T(1,128)} %bitcast.10), custom_call_target="tpu_custom_call" | custom-call | tf_op jit(solution)/shard_map/pallas_call | solution.py:384
  52.3 1.7 %shard_map.86 = (f32[256,128]{1,0:T(8,128)}, f32[256,128]{1,0:T(8,128)}, f32[16,16]{1,0:T(8,128)}) custom-call(f32[256,128]{1,0:T(8,128)} %get-tuple-element.9.a_ref, f32[256,128]{1,0:T(8,128)} %get-tuple-element.10.b_ref, f32[16,16]{1,0:T(8,128)} %get-tuple-element.11.c_ref), custom_call_target="tpu_custom_call" | custom-call | tf_op jit(solution)/shard_map/pallas_call | solution.py:444
